TPU v7x, 128 devices: a whole 4x4x4 slice. The times are simulated.
128 devices in a mesh: group: 4 (over x), cluster: 32 (over z, y, core).
Axes of the slice: x: 4, y: 4, z: 4, core: 2. Of those that a mesh axis runs over, the one named last changes fastest.
Arguments:
- charges: float32 [1048576, 128], P(('group', 'cluster')), may hold values from -6 to 6
- leaf_size: int32 [4096], P(('group', 'cluster')), may hold values from 1 to 256, 786432 in all
- leaf_basis: float32 [4096, 64, 256], P(('group', 'cluster')), may hold values from -0.375 to 0.375
- leaf_transfer: float32 [4096, 64, 64], P(('group', 'cluster')), may hold values from -0.375 to 0.375
- mid_transfer: float32 [1024, 64, 64], P(('group', 'cluster')), may hold values from -0.25 to 0.25
- leaf_parent: int32 [4096], P(('group', 'cluster')), may hold values from 0 to 7, as said below
- send_leaf: int32 [32768], P(('group', 'cluster')), may hold values from 0 to 32, as said below
- pair_leaf: int32 [4096, 12], P(('group', 'cluster')), may hold values from 0 to 256, as said below
- leaf_coupling: float32 [4096, 64, 768], P(('group', 'cluster')), may hold values from -0.21875 to 0.21875
- send_mid: int32 [32768], P(('group', 'cluster')), may hold values from 0 to 8, as said below
- pair_mid: int32 [1024, 32], P(('group', 'cluster')), may hold values from 0 to 256, as said below
- mid_coupling: float32 [1024, 64, 2048], P(('group', 'cluster')), may hold values from -0.125 to 0.125
- top_pairs: int32 [128, 4], P('group'), may hold values from 0 to 128, as said below
- top_coupling: float32 [128, 64, 256], P('group'), may hold values from -0.375 to 0.375
Outputs:
- far_field: float32 [1048576, 128], P(('group', 'cluster'))
Inputs may be any that keep to these rules, and one draw needn't show every extreme that they name: `send_leaf`: entry (d * 128 + r) * 2 + j is the leaf, local to device d, whose block d puts in slot j for device r, or 32 for an empty slot; the leaves in one sender's slots to one receiver are distinct; some receiver has every slot from every sender filled. `pair_leaf`: row t names leaf t's admissible partners as positions 2 * d + j among the slots its owner receives, filled slots only and distinct within a row, or 256 for no partner; every filled slot is named by some row of its receiver. `send_mid`: as send_leaf, for level-one clusters: local indices below 8, 8 for an empty slot; some receiver has every slot from every sender filled. `pair_mid`: as pair_leaf, for level-one clusters; every filled slot is named by some row of its receiver. `leaf_parent`: every level-one cluster of a device is the parent of at least one of its leaves. `top_pairs`: row o names coarse clusters other than o, distinct within a row, at least one a row, or 128 for no partner.
All inputs are finite; a program needn't handle non-finite values. No bound on the sum of `leaf_size` on one device may be relied on, other than what follows from the above.
Results may differ from a plain program's by a relative error of at most 0.000062.
Values sent between devices are 32-bit elements; how exact they have to be, the bound alone decides.
A program may use at most 128 MiB of HBM per device.

v0:
```python
import jax
import jax.numpy as jnp
from jax import lax
from jax.sharding import PartitionSpec as P

exact_mode = lax.Precision.HIGHEST


def couple(coupling, coef, index):
    stacked = jnp.take(coef, index, axis=0, mode="fill", fill_value=0.0)
    stacked = stacked.reshape(index.shape[0], index.shape[1] * coef.shape[1], coef.shape[2])
    return jnp.einsum("nkq,nqp->nkp", coupling, stacked, precision=exact_mode)


def body(
    charges,
    leaf_size,
    leaf_basis,
    leaf_transfer,
    mid_transfer,
    leaf_parent,
    send_leaf,
    pair_leaf,
    leaf_coupling,
    send_mid,
    pair_mid,
    mid_coupling,
    top_pairs,
    top_coupling,
):
    leaf_count, coef_rank, leaf_points = leaf_basis.shape
    port_count = charges.shape[1]
    mid_count = mid_transfer.shape[0]
    owners = send_leaf.shape[0] // 2
    slots = 2
    point_mask = (jnp.arange(leaf_points, dtype=jnp.int32)[None, :] < leaf_size[:, None]).astype(
        jnp.float32
    )
    blocks = charges.reshape(leaf_count, leaf_points, port_count) * point_mask[:, :, None]
    coef_leaf = jnp.einsum("lkm,lmp->lkp", leaf_basis, blocks, precision=exact_mode)
    moved_up = jnp.einsum("ljk,lkp->ljp", leaf_transfer, coef_leaf, precision=exact_mode)
    parent_map = (leaf_parent[None, :] == jnp.arange(mid_count, dtype=jnp.int32)[:, None]).astype(
        jnp.float32
    )
    coef_mid = jnp.einsum("ml,ljp->mjp", parent_map, moved_up, precision=exact_mode)
    coef_top = jnp.einsum("mjk,mkp->jp", mid_transfer, coef_mid, precision=exact_mode)
    outgoing_leaf = jnp.take(coef_leaf, send_leaf, axis=0, mode="fill", fill_value=0.0)
    outgoing_mid = jnp.take(coef_mid, send_mid, axis=0, mode="fill", fill_value=0.0)
    outgoing = jnp.concatenate(
        [
            outgoing_leaf.reshape(owners, slots, coef_rank, port_count),
            outgoing_mid.reshape(owners, slots, coef_rank, port_count),
        ],
        axis=1,
    ).reshape(owners * 2 * slots, coef_rank, port_count)
    arrived = lax.all_to_all(
        outgoing, ("group", "cluster"), split_axis=0, concat_axis=0, tiled=True
    )
    listed = top_pairs.shape[1]
    position = lax.axis_index("cluster")
    wanted = lax.dynamic_slice_in_dim(top_pairs, position, 1, 0)[0]
    own_coupling = lax.dynamic_slice_in_dim(top_coupling, position, 1, 0)[0]
    shard_rows = lax.all_gather(coef_top[None], ("group", "cluster"), axis=0, tiled=True)
    inside = (wanted >= 0) & (wanted < shard_rows.shape[0])
    taken_rows = jnp.take(shard_rows, jnp.clip(wanted, 0, shard_rows.shape[0] - 1), axis=0)
    picked = jnp.where(
        inside[:, None, None], taken_rows, jnp.zeros((listed, coef_rank, port_count), jnp.float32)
    )
    near_top = jnp.einsum(
        "kq,qp->kp",
        own_coupling,
        picked.reshape(listed * coef_rank, port_count),
        precision=exact_mode,
    )
    total_rows = owners * 2 * slots
    live_leaf = pair_leaf < owners * slots
    leaf_rows = jnp.where(live_leaf, pair_leaf + pair_leaf // slots * slots, total_rows)
    near_leaf = couple(leaf_coupling, arrived, leaf_rows)
    live_mid = pair_mid < owners * slots
    mid_rows = jnp.where(live_mid, pair_mid + (pair_mid // slots + 1) * slots, total_rows)
    near_mid = couple(mid_coupling, arrived, mid_rows)
    down_mid = near_mid + jnp.einsum("mjk,jp->mkp", mid_transfer, near_top, precision=exact_mode)
    from_parent = jnp.einsum("ml,mkp->lkp", parent_map, down_mid, precision=exact_mode)
    down_leaf = near_leaf + jnp.einsum(
        "ljk,ljp->lkp", leaf_transfer, from_parent, precision=exact_mode
    )
    far_field = (
        jnp.einsum("lkm,lkp->lmp", leaf_basis, down_leaf, precision=exact_mode)
        * point_mask[:, :, None]
    )
    return far_field.reshape(leaf_count * leaf_points, port_count)


def solution(mesh):
    in_specs = (
        P(("group", "cluster"), None),
        P(("group", "cluster")),
        P(("group", "cluster"), None, None),
        P(("group", "cluster"), None, None),
        P(("group", "cluster"), None, None),
        P(("group", "cluster")),
        P(("group", "cluster")),
        P(("group", "cluster"), None),
        P(("group", "cluster"), None, None),
        P(("group", "cluster")),
        P(("group", "cluster"), None),
        P(("group", "cluster"), None, None),
        P("group", None),
        P("group", None, None),
    )
    out_specs = P(("group", "cluster"), None)
    return jax.shard_map(body, mesh=mesh, in_specs=in_specs, out_specs=out_specs, check_vma=False)
```

profile of v0, /device:TPU:1, one launch (start us, length us, event | category | flops | bytes accessed | tf_op | source)
XLA Modules:
  0.0 382.9 jit_solution(8333064227275518542)
XLA Ops:
  6.5 0.8 compare_select_fusion.3
  7.4 0.7 compare_and_fusion.4
  8.1 0.7 compare_select_fusion.2
  8.7 0.7 compare_and_fusion.3
  9.4 0.7 fusion.11
  10.2 5.1 %fusion = f32[32,128,64]{1,2,0:T(8,128)S(1)} fusion(f32[32,64,256]{2,1,0:T(8,128)S(1)} %copy-done, f32[32,256,128]{2,1,0:T(8,128)} %bitcast.64, f32[32,256]{1,0:T(8,128)S(1)} %fusion.11), kind=kOutput, calls=%fused_computation.11 | convolution fusion | flops 806354944 | bytes 7372800 | tf_op jit(solution)/shard_map/lkm,lmp->lkp/dot_general | solution.py:40
  15.3 2.3 fusion.31
  17.6 1.0 fusion.4
  18.7 0.7 copy-done.4
  19.8 4.4 %gather_fusion.1 = f32[256,64,128]{2,1,0:T(8,128)} fusion(f32[8,64,128]{2,1,0:T(8,128)S(1)} %copy.19, s32[1024]{0:T(1024)S(1)} %pad_clamp_fusion.3), kind=kCustom, calls=%fused_computation.1 | custom fusion | bytes 16778240 | tf_op jit(solution)/shard_map/jit(_take)/gather | solution.py:48
  24.1 4.4 %gather_fusion = f32[256,64,128]{2,1,0:T(8,128)} fusion(f32[32,64,128]{2,1,0:T(8,128)S(1)} %bitcast.58, s32[1024]{0:T(1024)S(1)} %pad_clamp_fusion.4), kind=kCustom, calls=%fused_computation | custom fusion | bytes 16778240 | tf_op jit(solution)/shard_map/jit(_take)/gather | solution.py:47
  28.5 6.5 %broadcast_select_fusion = (f32[128,2,64,128]{3,2,1,0:T(8,128)S(1)}, f32[128,2,64,128]{3,2,1,0:T(8,128)S(1)}) fusion(f32[128,2,64,128]{3,2,1,0:T(8,128)} %bitcast.61, pred[128,2]{1,0:T(8,128)(4,1)S(1)} %broadcast_in_dim.105, f32[128,2,64,128]{3,2,1,0:T(8,128)} %bitcast.62, pred[128,2]{1,0:T(8,128)(4,1)S(1)} %broadcast_in_dim.101), kind=kLoop, calls=%fused_computation.9 | loop fusion | flops 4194304 | bytes 33554944 | tf_op jit(solution)/shard_map/jit(_take)/select_n | solution.py:48
  35.0 6.1 %pad_maximum_fusion = f32[128,4,64,128]{3,2,1,0:T(8,128)} fusion(f32[128,2,64,128]{3,2,1,0:T(8,128)S(1)} %get-tuple-element.9, f32[128,2,64,128]{3,2,1,0:T(8,128)S(1)} %get-tuple-element.10), kind=kLoop, calls=%fused_computation.5 | loop fusion | flops 4194304 | bytes 33554432 | tf_op jit(solution)/shard_map/concatenate | solution.py:49
  41.1 12.0 %all-to-all-start = ((f32[512,64,128]{2,1,0:T(8,128)}), f32[512,64,128]{2,1,0:T(8,128)}, u32[]{:S(2)}, u32[]{:S(2)}) async-start(f32[512,64,128]{2,1,0:T(8,128)} %bitcast.59), calls=%async_computation | async-start | bytes 33554432 | tf_op jit(solution)/shard_map/all_to_all | solution.py:56
  53.3 1.2 convolution_bitcast_fusion.3
  55.5 0.2 clamp_reduce_fusion
  55.7 0.2 and_reduce_fusion
  55.9 238.2 %all-gather.3.cloned.1.call-done = f32[8192,128]{1,0:T(8,128)} async-done(((f32[64,128]{1,0:T(8,128)}), f32[8192,128]{1,0:T(8,128)}) %all-gather.3.cloned.1.call-update) | async-done | bytes 4194320 | tf_op jit(solution)/shard_map/all_gather | solution.py:63
  294.1 2.7 gather_fusion.4
  297.0 1.1 convolution_bitcast_fusion.2
  298.1 1.4 convolution_bitcast_fusion.1
  299.5 10.1 %gather_fusion.3 = f32[256,64,128]{2,1,0:T(8,128)} fusion(f32[512,64,128]{2,1,0:T(8,128)} %all-to-all-done, s32[1024]{0:T(1024)S(1)} %pad_clamp_fusion.1), kind=kCustom, calls=%fused_computation.3 | custom fusion | bytes 16778240 | tf_op jit(solution)/shard_map/jit(_take)/gather | solution.py:10
  309.6 7.5 %bitcast_select_fusion.1 = f32[8,2048,128]{2,1,0:T(8,128)S(1)} fusion(pred[8,2048]{1,0:T(8,128)(4,1)S(1)} %broadcast_in_dim.112, f32[8,2048,128]{2,1,0:T(8,128)} %bitcast.63), kind=kLoop, calls=%fused_computation.7 | loop fusion | flops 2097152 | bytes 16793600 | tf_op jit(solution)/shard_map/jit(_take)/select_n | solution.py:10
  317.1 14.3 %fusion.3 = f32[8,64,128]{1,2,0:T(8,128)} fusion(f32[8,64,128]{1,2,0:T(8,128)S(1)} %copy-done.6, f32[8,2048,128]{2,1,0:T(8,128)S(1)} %bitcast_select_fusion.1, f32[8,64,2048]{2,1,0:T(8,128)S(1)} %copy-done.3), kind=kOutput, calls=%fused_computation.16 | convolution fusion | flops 1610678272 | bytes 13107200 | tf_op jit(solution)/shard_map/nkq,nqp->nkp/dot_general | solution.py:12
  331.4 1.2 copy.26
  332.6 0.6 fusion.23
  333.3 3.3 fusion.6
  336.6 11.7 %gather_fusion.2 = f32[384,64,128]{2,1,0:T(8,128)} fusion(f32[512,64,128]{2,1,0:T(8,128)} %all-to-all-done, s32[1024]{0:T(1024)S(1)} %pad_clamp_fusion.2), kind=kCustom, calls=%fused_computation.2 | custom fusion | bytes 25167360 | tf_op jit(solution)/shard_map/jit(_take)/gather | solution.py:10
  348.2 6.1 %bitcast_select_fusion = f32[32,768,128]{2,1,0:T(8,128)S(1)} fusion(pred[32,768]{1,0:T(8,128)(4,1)S(1)} %broadcast_in_dim.99, f32[32,768,128]{2,1,0:T(8,128)} %bitcast.60), kind=kLoop, calls=%fused_computation.6 | loop fusion | flops 3145728 | bytes 25190400 | tf_op jit(solution)/shard_map/jit(_take)/select_n | solution.py:10
  354.4 10.9 %convolution_add_fusion = f32[32,128,64]{1,2,0:T(8,128)S(1)} fusion(f32[32,128,64]{1,2,0:T(8,128)S(1)} %copy-done.2, f32[32,768,128]{2,1,0:T(8,128)S(1)} %bitcast_select_fusion, f32[32,64,768]{2,1,0:T(8,128)} %param.22), kind=kOutput, calls=%fused_computation.14 | convolution fusion | flops 2416181248 | bytes 20971520 | tf_op jit(solution)/shard_map/nkq,nqp->nkp/dot_general | solution.py:12
  365.3 5.2 %multiply_bitcast_fusion = f32[32,256,128]{1,2,0:T(8,128)} fusion(f32[32,128,64]{1,2,0:T(8,128)S(1)} %convolution_add_fusion, f32[32,64,256]{2,1,0:T(8,128)S(1)} %copy-done, f32[32,256]{1,0:T(8,128)S(1)} %fusion.11), kind=kOutput, calls=%fused_computation.8 | convolution fusion | flops 806354944 | bytes 7372800 | tf_op jit(solution)/shard_map/lkm,lkp->lmp/dot_general | solution.py:88
  370.5 5.6 %copy.22 = f32[32,256,128]{2,1,0:T(8,128)} copy(f32[32,256,128]{1,2,0:T(8,128)} %multiply_bitcast_fusion) | data formatting | bytes 8388608 | tf_op jit(solution)/shard_map/mul | solution.py:88
  (48 shorter events, 1.6 us)
Async XLA Ops:
  6.5 3.6 copy-start
  6.5 11.1 %copy-start.11 = (s32[32]{0:T(128)S(1)}, s32[32]{0:T(128)}, u32[]{:S(2)}) copy-start(s32[32]{0:T(128)} %param.19) | copy-start | bytes 388
  18.6 0.7 copy-start.4
  41.1 12.0 %copy-start.7 = (f32[8,64,64]{2,1,0:T(8,128)S(1)}, f32[8,64,64]{2,1,0:T(8,128)}, u32[]{:S(2)}) copy-start(f32[8,64,64]{2,1,0:T(8,128)} %param.18) | copy-start | bytes 393220
  41.1 12.2 %copy-start.5 = (f32[8,64,128]{2,0,1:T(8,128)S(1)}, f32[8,64,128]{2,0,1:T(8,128)}, u32[]{:S(2)}) copy-start(f32[8,64,128]{2,0,1:T(8,128)} %copy-done.4) | copy-start | bytes 786436
  41.1 13.4 %copy-start.10 = (s32[8,32]{1,0:T(8,128)S(1)}, s32[8,32]{1,0:T(8,128)}, u32[]{:S(2)}) copy-start(s32[8,32]{1,0:T(8,128)} %param.24) | copy-start | bytes 3076
  41.1 13.8 %copy-start.9 = (s32[32,12]{0,1:T(8,128)S(1)}, s32[32,12]{0,1:T(8,128)}, u32[]{:S(2)}) copy-start(s32[32,12]{0,1:T(8,128)} %param.21) | copy-start | bytes 4612
  41.1 14.4 %copy-start.8 = (s32[32,4]{0,1:T(4,128)S(1)}, s32[32,4]{0,1:T(4,128)}, u32[]{:S(2)}) copy-start(s32[32,4]{0,1:T(4,128)} %param.26) | copy-start | bytes 1540
  41.1 258.4 %all-to-all-start = ((f32[512,64,128]{2,1,0:T(8,128)}), f32[512,64,128]{2,1,0:T(8,128)}, u32[]{:S(2)}, u32[]{:S(2)}) async-start(f32[512,64,128]{2,1,0:T(8,128)} %bitcast.59), calls=%async_computation | async-start | bytes 33554432 | tf_op jit(solution)/shard_map/all_to_all | solution.py:56
  53.1 241.1 %all-gather.3.cloned.1.call-start = ((), (), s32[]{:S(2)}) async-start(), calls=%async_computation.1 | async-start | bytes 4227072 | tf_op jit(solution)/shard_map/all_gather | solution.py:63
  309.6 7.5 %copy-start.3 = (f32[8,64,2048]{2,1,0:T(8,128)S(1)}, f32[8,64,2048]{2,1,0:T(8,128)}, u32[]{:S(2)}) copy-start(f32[8,64,2048]{2,1,0:T(8,128)} %param.25) | copy-start | bytes 12582916
  309.6 7.5 %copy-start.6 = (f32[8,64,128]{1,2,0:T(8,128)S(1)}, f32[8,64,128]{1,2,0:T(8,128)}, u32[]{:S(2)}) copy-start(f32[8,64,128]{1,2,0:T(8,128)} %convolution_bitcast_fusion.1) | copy-start | bytes 786436
  317.1 16.2 %copy-start.1 = (f32[32,64,64]{2,1,0:T(8,128)S(1)}, f32[32,64,64]{2,1,0:T(8,128)}, u32[]{:S(2)}) copy-start(f32[32,64,64]{2,1,0:T(8,128)} %param.17) | copy-start | bytes 1572868
  348.2 6.1 %copy-start.2 = (f32[32,128,64]{1,2,0:T(8,128)S(1)}, f32[32,128,64]{1,2,0:T(8,128)}, u32[]{:S(2)}) copy-start(f32[32,128,64]{1,2,0:T(8,128)} %fusion.6) | copy-start | bytes 3145732
Sparse Core Ops, SparseCore 0:
  57.1 237.0 all-gather.2
where the time goes:
time: 384 us; the launch traced here: 383 us
  waiting for transfers between devices  238 us (62%)
  matrix products  46.5 us (12%)
  local copies, waits for them, and re-layouts  42.1 us (11%)
  other arithmetic  30.3 us (8%)
  between operations  13.7 us (4%)
  starting transfers between devices  12 us (3%)
    all_gather x1, waiting for transfers between devices, body(): lax.all_gather(coef_top[None], ('group', 'cluster'), axis=0, tiled=True)  238 us
    dot_general x2, matrix products, couple(): return jnp.einsum('nkq,nqp->nkp', coupling, stacked, precision=exact_mode)  25.2 us
    gather x2, local copies, waits for them, and re-layouts, couple(): stacked = jnp.take(coef, index, axis=0, mode='fill', fill_value=0.0)  21.8 us
    select_n x2, other arithmetic, couple(): stacked = jnp.take(coef, index, axis=0, mode='fill', fill_value=0.0)  13.6 us
    all_to_all x1, starting transfers between devices, body(): lax.all_to_all(outgoing, ('group', 'cluster'), split_axis=0, concat_axis=...  12 us
  transfers between devices with their start and end apart: 2, of which 1 were waited for; matrix products, arithmetic and copies ran while one was open for 2% of the time, Pallas kernels for 0%

commit v1 on v0

--- a/solution.py
+++ b/solution.py
@@ -60,7 +60,15 @@
     position = lax.axis_index("cluster")
     wanted = lax.dynamic_slice_in_dim(top_pairs, position, 1, 0)[0]
     own_coupling = lax.dynamic_slice_in_dim(top_coupling, position, 1, 0)[0]
-    shard_rows = lax.all_gather(coef_top[None], ("group", "cluster"), axis=0, tiled=True)
+    shard_rows = jnp.concatenate(
+        lax.all_to_all(
+            jnp.stack([coef_top[None]] * lax.axis_size(("group", "cluster"))),
+            ("group", "cluster"),
+            0,
+            0,
+        ),
+        axis=0,
+    )
     inside = (wanted >= 0) & (wanted < shard_rows.shape[0])
     taken_rows = jnp.take(shard_rows, jnp.clip(wanted, 0, shard_rows.shape[0] - 1), axis=0)
     picked = jnp.where(

time: 384 us -> 403 us (1.049)
  the two profiles are of different devices: /device:TPU:1 before, /device:TPU:98 now
where the time goes in v1:
time: 403 us; the launch traced here: 402 us
  waiting for transfers between devices  262 us (65%)
  local copies, waits for them, and re-layouts  46.6 us (12%)
  matrix products  45.9 us (11%)
  other arithmetic  27.6 us (7%)
  starting transfers between devices  19.3 us (5%)
    all_to_all x1, waiting for transfers between devices, body(): lax.all_to_all(outgoing, ('group', 'cluster'), split_axis=0, concat_axis=...  235 us
    all_to_all x1, waiting for transfers between devices, body(): lax.all_to_all(jnp.stack([coef_top[None]] * lax.axis_size(('group', 'clus...  27 us
    dot_general x2, matrix products, couple(): return jnp.einsum('nkq,nqp->nkp', coupling, stacked, precision=exact_mode)  25.2 us
    gather x2, local copies, waits for them, and re-layouts, couple(): stacked = jnp.take(coef, index, axis=0, mode='fill', fill_value=0.0)  21.8 us
    select_n x2, other arithmetic, couple(): stacked = jnp.take(coef, index, axis=0, mode='fill', fill_value=0.0)  13.6 us
    all_to_all x1, starting transfers between devices, body(): lax.all_to_all(jnp.stack([coef_top[None]] * lax.axis_size(('group', 'clus...  10.3 us
    all_to_all x1, starting transfers between devices, body(): lax.all_to_all(outgoing, ('group', 'cluster'), split_axis=0, concat_axis=...  9.03 us
  transfers between devices with their start and end apart: 2, of which 2 were waited for; matrix products, arithmetic and copies ran while one was open for 7% of the time, Pallas kernels for 0%

profile of v1, /device:TPU:98, one launch (start us, length us, event | category | flops | bytes accessed | tf_op | source)
XLA Modules:
  0.0 402.0 jit_solution(11334456449263422739)
XLA Ops:
  0.0 0.9 fusion.11
  0.9 1.1 copy.25
  2.0 5.1 %fusion = f32[32,128,64]{1,2,0:T(8,128)S(1)} fusion(f32[32,64,256]{2,1,0:T(8,128)S(1)} %copy-done, f32[32,256,128]{2,1,0:T(8,128)} %bitcast.64, f32[32,256]{1,0:T(8,128)S(1)} %fusion.11), kind=kOutput, calls=%fused_computation.11 | convolution fusion | flops 806354944 | bytes 7372800 | tf_op jit(solution)/shard_map/lkm,lmp->lkp/dot_general | solution.py:40
  7.1 2.3 fusion.31
  9.5 1.0 fusion.4
  10.5 0.7 copy-done.4
  11.2 0.6 convolution_bitcast_fusion.3
  11.8 2.5 stack.3
  14.4 10.3 %all-to-all-start.1 = ((f32[128,1,64,128]{3,2,1,0:T(8,128)}), f32[128,1,64,128]{3,2,1,0:T(8,128)}, u32[]{:S(2)}, u32[]{:S(2)}) async-start(f32[128,1,64,128]{3,2,1,0:T(8,128)} %stack.3), calls=%async_computation.1 | async-start | bytes 8388608 | tf_op jit(solution)/shard_map/all_to_all | solution.py:64
  24.7 1.0 copy.19
  26.1 4.4 %gather_fusion.1 = f32[256,64,128]{2,1,0:T(8,128)} fusion(f32[8,64,128]{2,1,0:T(8,128)S(1)} %copy.19, s32[1024]{0:T(1024)S(1)} %pad_clamp_fusion.3), kind=kCustom, calls=%fused_computation.1 | custom fusion | bytes 16778240 | tf_op jit(solution)/shard_map/jit(_take)/gather | solution.py:48
  30.4 4.4 %gather_fusion = f32[256,64,128]{2,1,0:T(8,128)} fusion(f32[32,64,128]{2,1,0:T(8,128)S(1)} %bitcast.58, s32[1024]{0:T(1024)S(1)} %pad_clamp_fusion.4), kind=kCustom, calls=%fused_computation | custom fusion | bytes 16778240 | tf_op jit(solution)/shard_map/jit(_take)/gather | solution.py:47
  34.8 6.5 %broadcast_select_fusion = (f32[128,2,64,128]{3,2,1,0:T(8,128)S(1)}, f32[128,2,64,128]{3,2,1,0:T(8,128)S(1)}) fusion(f32[128,2,64,128]{3,2,1,0:T(8,128)} %bitcast.61, pred[128,2]{1,0:T(8,128)(4,1)S(1)} %broadcast_in_dim.102, f32[128,2,64,128]{3,2,1,0:T(8,128)} %bitcast.62, pred[128,2]{1,0:T(8,128)(4,1)S(1)} %broadcast_in_dim.98), kind=kLoop, calls=%fused_computation.9 | loop fusion | flops 4194304 | bytes 33554944 | tf_op jit(solution)/shard_map/jit(_take)/select_n | solution.py:48
  41.4 6.1 %pad_maximum_fusion = f32[128,4,64,128]{3,2,1,0:T(8,128)} fusion(f32[128,2,64,128]{3,2,1,0:T(8,128)S(1)} %get-tuple-element.9, f32[128,2,64,128]{3,2,1,0:T(8,128)S(1)} %get-tuple-element.10), kind=kLoop, calls=%fused_computation.5 | loop fusion | flops 4194304 | bytes 33554432 | tf_op jit(solution)/shard_map/concatenate | solution.py:49
  47.4 27.0 %all-to-all-done.1 = f32[128,1,64,128]{3,2,1,0:T(8,128)} async-done(((f32[128,1,64,128]{3,2,1,0:T(8,128)}), f32[128,1,64,128]{3,2,1,0:T(8,128)}, u32[]{:S(2)}, u32[]{:S(2)}) %all-to-all-start.1) | async-done | bytes 4194336 | tf_op jit(solution)/shard_map/all_to_all | solution.py:64
  74.5 9.0 %all-to-all-start = ((f32[512,64,128]{2,1,0:T(8,128)}), f32[512,64,128]{2,1,0:T(8,128)}, u32[]{:S(2)}, u32[]{:S(2)}) async-start(f32[512,64,128]{2,1,0:T(8,128)} %bitcast.59), calls=%async_computation | async-start | bytes 33554432 | tf_op jit(solution)/shard_map/all_to_all | solution.py:56
  84.5 0.2 clamp_reduce_fusion
  84.9 2.7 gather_fusion.4
  87.7 1.1 convolution_bitcast_fusion.2
  88.8 1.4 convolution_bitcast_fusion.1
  90.2 235.2 %all-to-all-done = f32[512,64,128]{2,1,0:T(8,128)} async-done(((f32[512,64,128]{2,1,0:T(8,128)}), f32[512,64,128]{2,1,0:T(8,128)}, u32[]{:S(2)}, u32[]{:S(2)}) %all-to-all-start) | async-done | bytes 16777248 | tf_op jit(solution)/shard_map/all_to_all | solution.py:56
  325.4 10.1 %gather_fusion.3 = f32[256,64,128]{2,1,0:T(8,128)} fusion(f32[512,64,128]{2,1,0:T(8,128)} %all-to-all-done, s32[1024]{0:T(1024)S(1)} %pad_clamp_fusion.1), kind=kCustom, calls=%fused_computation.3 | custom fusion | bytes 16778240 | tf_op jit(solution)/shard_map/jit(_take)/gather | solution.py:10
  335.5 7.5 %bitcast_select_fusion.1 = f32[8,2048,128]{2,1,0:T(8,128)S(1)} fusion(pred[8,2048]{1,0:T(8,128)(4,1)S(1)} %broadcast_in_dim.109, f32[8,2048,128]{2,1,0:T(8,128)} %bitcast.63), kind=kLoop, calls=%fused_computation.7 | loop fusion | flops 2097152 | bytes 16793600 | tf_op jit(solution)/shard_map/jit(_take)/select_n | solution.py:10
  343.0 14.3 %fusion.3 = f32[8,64,128]{1,2,0:T(8,128)} fusion(f32[8,64,128]{1,2,0:T(8,128)S(1)} %copy-done.5, f32[8,2048,128]{2,1,0:T(8,128)S(1)} %bitcast_select_fusion.1, f32[8,64,2048]{2,1,0:T(8,128)S(1)} %copy-done.3), kind=kOutput, calls=%fused_computation.16 | convolution fusion | flops 1610678272 | bytes 13107200 | tf_op jit(solution)/shard_map/nkq,nqp->nkp/dot_general | solution.py:12
  357.3 1.2 copy.26
  358.5 0.6 fusion.23
  359.2 3.3 fusion.6
  362.5 11.7 %gather_fusion.2 = f32[384,64,128]{2,1,0:T(8,128)} fusion(f32[512,64,128]{2,1,0:T(8,128)} %all-to-all-done, s32[1024]{0:T(1024)S(1)} %pad_clamp_fusion.2), kind=kCustom, calls=%fused_computation.2 | custom fusion | bytes 25167360 | tf_op jit(solution)/shard_map/jit(_take)/gather | solution.py:10
  374.2 6.1 %bitcast_select_fusion = f32[32,768,128]{2,1,0:T(8,128)S(1)} fusion(pred[32,768]{1,0:T(8,128)(4,1)S(1)} %broadcast_in_dim.96, f32[32,768,128]{2,1,0:T(8,128)} %bitcast.60), kind=kLoop, calls=%fused_computation.6 | loop fusion | flops 3145728 | bytes 25190400 | tf_op jit(solution)/shard_map/jit(_take)/select_n | solution.py:10
  380.3 10.9 %convolution_add_fusion = f32[32,128,64]{1,2,0:T(8,128)S(1)} fusion(f32[32,128,64]{1,2,0:T(8,128)S(1)} %copy-done.2, f32[32,768,128]{2,1,0:T(8,128)S(1)} %bitcast_select_fusion, f32[32,64,768]{2,1,0:T(8,128)} %param.22), kind=kOutput, calls=%fused_computation.14 | convolution fusion | flops 2416181248 | bytes 20971520 | tf_op jit(solution)/shard_map/nkq,nqp->nkp/dot_general | solution.py:12
  391.2 5.2 %multiply_bitcast_fusion = f32[32,256,128]{1,2,0:T(8,128)} fusion(f32[32,128,64]{1,2,0:T(8,128)S(1)} %convolution_add_fusion, f32[32,64,256]{2,1,0:T(8,128)S(1)} %copy-done, f32[32,256]{1,0:T(8,128)S(1)} %fusion.11), kind=kOutput, calls=%fused_computation.8 | convolution fusion | flops 806354944 | bytes 7372800 | tf_op jit(solution)/shard_map/lkm,lkp->lmp/dot_general | solution.py:96
  396.5 5.6 %copy.22 = f32[32,256,128]{2,1,0:T(8,128)} copy(f32[32,256,128]{1,2,0:T(8,128)} %multiply_bitcast_fusion) | data formatting | bytes 8388608 | tf_op jit(solution)/shard_map/mul | solution.py:96
  (50 shorter events, 1.6 us)
Async XLA Ops:
  0.0 2.0 copy-start
  0.0 9.5 %copy-start.10 = (s32[32]{0:T(128)S(1)}, s32[32]{0:T(128)}, u32[]{:S(2)}) copy-start(s32[32]{0:T(128)} %param.19) | copy-start | bytes 388
  7.1 18.6 %copy-start.11 = (s32[256]{0:T(256)S(1)}, s32[256]{0:T(256)}, u32[]{:S(2)}) copy-start(s32[256]{0:T(256)} %param.23) | copy-start | bytes 3076
  7.1 18.7 %copy-start.12 = (s32[256]{0:T(256)S(1)}, s32[256]{0:T(256)}, u32[]{:S(2)}) copy-start(s32[256]{0:T(256)} %param.20) | copy-start | bytes 3076
  10.5 0.7 copy-start.4
  14.4 60.1 %all-to-all-start.1 = ((f32[128,1,64,128]{3,2,1,0:T(8,128)}), f32[128,1,64,128]{3,2,1,0:T(8,128)}, u32[]{:S(2)}, u32[]{:S(2)}) async-start(f32[128,1,64,128]{3,2,1,0:T(8,128)} %stack.3), calls=%async_computation.1 | async-start | bytes 8388608 | tf_op jit(solution)/shard_map/all_to_all | solution.py:64
  74.5 9.1 %copy-start.9 = (s32[8,32]{1,0:T(8,128)S(1)}, s32[8,32]{1,0:T(8,128)}, u32[]{:S(2)}) copy-start(s32[8,32]{1,0:T(8,128)} %param.24) | copy-start | bytes 3076
  74.5 9.4 %copy-start.8 = (s32[32,12]{0,1:T(8,128)S(1)}, s32[32,12]{0,1:T(8,128)}, u32[]{:S(2)}) copy-start(s32[32,12]{0,1:T(8,128)} %param.21) | copy-start | bytes 4612
  74.5 10.0 %copy-start.7 = (s32[32,4]{0,1:T(4,128)S(1)}, s32[32,4]{0,1:T(4,128)}, u32[]{:S(2)}) copy-start(s32[32,4]{0,1:T(4,128)} %param.26) | copy-start | bytes 1540
  74.5 14.3 %copy-start.6 = (f32[8,64,64]{2,1,0:T(8,128)S(1)}, f32[8,64,64]{2,1,0:T(8,128)}, u32[]{:S(2)}) copy-start(f32[8,64,64]{2,1,0:T(8,128)} %param.18) | copy-start | bytes 393220
  74.5 250.9 %all-to-all-start = ((f32[512,64,128]{2,1,0:T(8,128)}), f32[512,64,128]{2,1,0:T(8,128)}, u32[]{:S(2)}, u32[]{:S(2)}) async-start(f32[512,64,128]{2,1,0:T(8,128)} %bitcast.59), calls=%async_computation | async-start | bytes 33554432 | tf_op jit(solution)/shard_map/all_to_all | solution.py:56
  335.5 7.5 %copy-start.3 = (f32[8,64,2048]{2,1,0:T(8,128)S(1)}, f32[8,64,2048]{2,1,0:T(8,128)}, u32[]{:S(2)}) copy-start(f32[8,64,2048]{2,1,0:T(8,128)} %param.25) | copy-start | bytes 12582916
  335.5 7.5 %copy-start.5 = (f32[8,64,128]{1,2,0:T(8,128)S(1)}, f32[8,64,128]{1,2,0:T(8,128)}, u32[]{:S(2)}) copy-start(f32[8,64,128]{1,2,0:T(8,128)} %convolution_bitcast_fusion.1) | copy-start | bytes 786436
  343.0 16.2 %copy-start.1 = (f32[32,64,64]{2,1,0:T(8,128)S(1)}, f32[32,64,64]{2,1,0:T(8,128)}, u32[]{:S(2)}) copy-start(f32[32,64,64]{2,1,0:T(8,128)} %param.17) | copy-start | bytes 1572868
  374.2 6.1 %copy-start.2 = (f32[32,128,64]{1,2,0:T(8,128)S(1)}, f32[32,128,64]{1,2,0:T(8,128)}, u32[]{:S(2)}) copy-start(f32[32,128,64]{1,2,0:T(8,128)} %fusion.6) | copy-start | bytes 3145732
